TPU v7x, 32 devices: a whole 2x2x4 slice. The times are simulated.
32 devices in a mesh: grp: 2 (over core), mr: 8 (over z, y), mc: 2 (over x).
Axes of the slice: x: 2, y: 2, z: 4, core: 2. Of those that a mesh axis runs over, the one named last changes fastest.
Arguments:
- queries: bfloat16 [384, 8192], P(('grp', 'mr'), 'mc'), may hold values from -6 to 6
- new_keys: bfloat16 [384, 1024], P(('grp', 'mr'), 'mc'), may hold values from -6 to 6
- new_values: bfloat16 [384, 1024], P(('grp', 'mr'), 'mc'), may hold values from -6 to 6
- key_cache: bfloat16 [384, 512, 1024], P(('grp', 'mr'), None, 'mc'), may hold values from -6 to 6
- value_cache: bfloat16 [384, 512, 1024], P(('grp', 'mr'), None, 'mc'), may hold values from -6 to 6
- context_len: int32 [384], P(('grp', 'mr')), may hold values from 2 to 512, as said below
- cache_slot: int32 [384], P(('grp', 'mr')), may hold values from 0 to 383, as said below
- residual_in: bfloat16 [384, 8192], P(('grp', 'mr'), 'mc'), may hold values from -31 to 31
- out_weight: bfloat16 [8192, 8192], P(('grp', 'mr'), 'mc'), may hold values from -0.25 to 0.25
- gate_weight: bfloat16 [8192, 28672], P('mc', ('grp', 'mr')), may hold values from -0.0625 to 0.0625
- up_weight: bfloat16 [8192, 28672], P('mc', ('grp', 'mr')), may hold values from -0.0625 to 0.0625
Outputs:
- residual_out: bfloat16 [384, 8192], P(('grp', 'mr'), 'mc')
- activation: bfloat16 [384, 28672], P('mc', ('grp', 'mr'))
Inputs may be any that keep to these rules, and one draw needn't show every extreme that they name: Row r's history fills positions 0 to context_len[r] - 1 of its cache row; some row has 512. `cache_slot`: within each aligned block of 24 rows the values are a permutation of that block's own row indices.
All inputs are finite; a program needn't handle non-finite values.
Results may differ from a plain program's by a relative error of at most 0.006.
Values may be sent and summed in bfloat16 or wider, within the bound.
A program may use at most 128 MiB of HBM per device.

v0:
```python
import jax
import jax.numpy as jnp
from jax import lax
from jax.sharding import PartitionSpec as P

D = 8192
HD = 128


norm_epsilon = 1e-05
masked_score = -1e30


def attend_rows(queries, new_keys, new_values, key_rows, value_rows, context_len):
    row_denominator_sum = queries.shape[0]
    context = key_rows.shape[1]
    kv_heads = key_rows.shape[2] // HD
    groups = queries.shape[1] // key_rows.shape[2]
    attention_logit_scale = HD ** (-0.5)
    query_grouped_four = queries.reshape(row_denominator_sum, kv_heads, groups, HD)
    key_four = key_rows.reshape(row_denominator_sum, context, kv_heads, HD)
    value_four = value_rows.reshape(row_denominator_sum, context, kv_heads, HD)
    current_key = new_keys.reshape(row_denominator_sum, kv_heads, HD)
    own_value = new_values.reshape(row_denominator_sum, kv_heads, HD).astype(jnp.float32)
    scores = (
        jnp.einsum(
            "bkgd,bckd->bkgc", query_grouped_four, key_four, preferred_element_type=jnp.float32
        )
        * attention_logit_scale
    )
    positions = jnp.arange(context, dtype=jnp.int32)
    valid_mask = positions[None, :] < context_len[:, None]
    scores = jnp.where(valid_mask[:, None, None, :], scores, masked_score)
    current_score = (
        jnp.einsum(
            "cnhz,cnz->cnh", query_grouped_four, current_key, preferred_element_type=jnp.float32
        )
        * attention_logit_scale
    )
    row_max = jnp.maximum(jnp.max(scores, axis=3), current_score)
    exponent = jnp.exp(scores - row_max[..., None])
    own_exponent = jnp.exp(current_score - row_max)
    denominator = jnp.sum(exponent, axis=3) + own_exponent
    weights = (exponent / denominator[..., None]).astype(jnp.bfloat16)
    own_weight = (own_exponent / denominator).astype(jnp.bfloat16).astype(jnp.float32)
    combined = jnp.einsum(
        "bkgc,bckd->bkgd", weights, value_four, preferred_element_type=jnp.float32
    )
    combined = combined + own_weight[..., None] * own_value[:, :, None, :]
    return combined.reshape(row_denominator_sum, -1).astype(jnp.bfloat16)


def body(
    queries,
    new_keys,
    new_values,
    key_cache,
    value_cache,
    context_len,
    cache_slot,
    residual_in,
    out_weight,
    gate_weight,
    up_weight,
):
    local_rows = queries.shape[0]
    row_base = lax.axis_index(("grp", "mr")) * local_rows
    device_slot_index = cache_slot - row_base
    positions = jnp.arange(local_rows, dtype=jnp.int32)
    matches = device_slot_index[:, None] == positions[None, :]
    inverse = jnp.sum(jnp.where(matches, positions[:, None], 0), axis=0)
    by_cache = attend_rows(
        jnp.take(queries, inverse, axis=0),
        jnp.take(new_keys, inverse, axis=0),
        jnp.take(new_values, inverse, axis=0),
        key_cache,
        value_cache,
        jnp.take(context_len, inverse, axis=0),
    )
    attended = jnp.take(by_cache, device_slot_index, axis=0)
    gathered = lax.all_gather(attended, "mc", axis=1, tiled=True)
    features = lax.all_to_all(gathered, ("grp", "mr"), split_axis=1, concat_axis=0, tiled=True)
    shares = lax.psum_scatter(
        jnp.dot(features, out_weight, preferred_element_type=jnp.float32),
        ("grp", "mr"),
        scatter_dimension=0,
        tiled=True,
    )
    residual_out = (residual_in.astype(jnp.float32) + shares).astype(jnp.bfloat16)
    everyone = lax.all_gather(residual_out, ("grp", "mr"), axis=0, tiled=True)
    widened = lax.optimization_barrier(everyone).astype(jnp.float32)
    squares = jnp.sum(widened * widened, axis=1)
    gate_term = jnp.dot(everyone, gate_weight, preferred_element_type=jnp.float32)
    up_term = jnp.dot(everyone, up_weight, preferred_element_type=jnp.float32)
    gate_sum, up_sum, square_sum = (
        lax.psum_scatter(gate_term, "mc", scatter_dimension=0, tiled=True),
        lax.psum_scatter(up_term, "mc", scatter_dimension=0, tiled=True),
        lax.psum_scatter(squares, "mc", scatter_dimension=0, tiled=True),
    )
    inverse_rms = lax.rsqrt(square_sum / D + norm_epsilon)
    gate_value = gate_sum * inverse_rms[:, None]
    upward = up_sum * inverse_rms[:, None]
    activation = (jax.nn.silu(gate_value) * upward).astype(jnp.bfloat16)
    return (residual_out, activation)


def solution(mesh):
    in_specs = (
        P(("grp", "mr"), "mc"),
        P(("grp", "mr"), "mc"),
        P(("grp", "mr"), "mc"),
        P(("grp", "mr"), None, "mc"),
        P(("grp", "mr"), None, "mc"),
        P(("grp", "mr")),
        P(("grp", "mr")),
        P(("grp", "mr"), "mc"),
        P(("grp", "mr"), "mc"),
        P("mc", ("grp", "mr")),
        P("mc", ("grp", "mr")),
    )
    out_specs = (P(("grp", "mr"), "mc"), P("mc", ("grp", "mr")))
    return jax.shard_map(body, mesh=mesh, in_specs=in_specs, out_specs=out_specs, check_vma=False)
```

profile of v0, /device:TPU:0, one launch (start us, length us, event | category | flops | bytes accessed | tf_op | source)
XLA Modules:
  0.0 293.3 jit_solution(18301695469659313411)
XLA Ops:
  7.2 0.0 copy-start
  7.2 0.0 reduce-scatter.4.cloned.1.call-start
  7.2 0.7 compare_and_fusion
  7.9 0.1 select_reduce_fusion
  8.1 1.4 gather_fusion
  9.4 1.4 gather_fusion.2
  10.8 1.4 gather_fusion.3
  12.1 0.1 select_convert_fusion
  12.3 0.0 copy-done
  12.3 0.7 gather_fusion.1
  12.9 0.1 select_bitcast_fusion
  13.1 0.1 iota_compare_fusion
  13.1 0.2 fusion.23
  13.4 6.4 %fusion.22 = (f32[24,4,8]{2,1,0:T(4,128)S(1)}, f32[24,4,8,512]{3,2,1,0:T(8,128)S(1)}) fusion(bf16[24,4,8,128]{3,2,1,0:T(8,128)(2,1)S(1)} %bitcast.59, pred[24,512]{1,0:T(8,128)(4,1)S(1)} %iota_compare_fusion, bf16[24,512,512]{2,1,0:T(8,128)(2,1)} %param.18), kind=kOutput, calls=%fused_computation.50 | convolution fusion | flops 101842176 | bytes 14367744 | tf_op jit(solution)/shard_map/bkgd,bckd->bkgc/dot_general | solution.py:26
  19.9 0.5 fusion.8
  20.5 5.8 %fusion.12 = bf16[24,4,8,128]{3,2,1,0:T(8,128)(2,1)S(1)} fusion(f32[24,4,8,512]{3,2,1,0:T(8,128)S(1)} %get-tuple-element.14, f32[24,4,8]{2,1,0:T(4,128)S(1)} %get-tuple-element.9, f32[24,4,8]{2,1,0:T(4,128)S(1)} %multiply_maximum_fusion, f32[24,4,128]{2,1,0:T(4,128)S(1)} %reshape.91, f32[24,4,8]{2,1,0:T(4,128)S(1)} %get-tuple-element.8, ...), kind=kOutput, calls=%fused_computation.18 | convolution fusion | flops 102137856 | bytes 14410752 | tf_op jit(solution)/shard_map/bkgc,bckd->bkgd/dot_general | solution.py:46
  26.2 0.1 copy.50
  26.3 0.7 gather_fusion.4
  27.0 0.1 broadcast_select_fusion
  27.1 8.5 %all_gather.6 = bf16[24,8192]{1,0:T(8,128)(2,1)S(1)} all-gather(bf16[24,4096]{1,0:T(8,128)(2,1)S(1)} %broadcast_select_fusion), channel_id=1, replica_groups=mesh['grp'=2,'mr'=8,'mc'=2] {'mc'}, dimensions={1}, use_global_device_ids=true | all-gather | bytes 589824 | tf_op jit(solution)/shard_map/all_gather | solution.py:81
  35.7 19.0 %all_to_all.19 = bf16[24,16,512]{2,0,1:T(8,128)(2,1)S(1)} all-to-all(bf16[24,16,512]{2,0,1:T(8,128)(2,1)S(1)} %bitcast.56), channel_id=1, replica_groups=mesh['grp'=2,'mr'=8,'mc'=2] {'grp','mr'}, dimensions={1} | all-to-all | bytes 786432 | tf_op jit(solution)/shard_map/all_to_all | solution.py:82
  54.7 6.6 %fusion.24 = f32[384,4096]{1,0:T(8,128)} fusion(bf16[384,512]{1,0:T(8,128)(2,1)S(1)} %bitcast.57, bf16[512,4096]{1,0:T(8,128)(2,1)} %param.23), kind=kOutput, calls=%fused_computation.52 | convolution fusion | flops 1610612736 | bytes 10878976 | tf_op jit(solution)/shard_map/dot_general | solution.py:84
  61.4 0.0 copy-start.3
  61.4 0.0 reduce-scatter.4.cloned.1.call-update
  61.4 0.0 all-gather.2.cloned.1.call-start
  61.4 83.0 %reduce-scatter.4.cloned.1.call-done = f32[24,4096]{1,0:T(8,128)} async-done(((f32[384,4096]{1,0:T(8,128)}), f32[24,4096]{1,0:T(8,128)}) %reduce-scatter.4.cloned.1.call-update) | async-done | bytes 393232 | tf_op jit(solution)/shard_map/reduce_scatter | solution.py:83
  144.4 0.0 copy-done.3
  144.4 1.7 add_convert_fusion
  146.1 0.0 all-gather.2.cloned.1.call-update
  146.1 0.0 reduce-scatter.6.cloned.1.call-start
  146.2 45.6 %all-gather.2.cloned.1.call-done = bf16[384,4096]{1,0:T(8,128)(2,1)} async-done(((bf16[24,4096]{1,0:T(8,128)(2,1)}), bf16[384,4096]{1,0:T(8,128)(2,1)}) %all-gather.2.cloned.1.call-update) | async-done | bytes 3145744 | tf_op jit(solution)/shard_map/all_gather | solution.py:90
  191.8 0.0 copy-start.2
  191.8 12.9 %fusion.25 = f32[384,1792]{1,0:T(8,128)} fusion(bf16[384,4096]{1,0:T(8,128)(2,1)} %all-gather.2.cloned.1.call-done, bf16[4096,1792]{1,0:T(8,128)(2,1)} %param.24), kind=kOutput, calls=%fused_computation.53 | convolution fusion | flops 5637144576 | bytes 20578304 | tf_op jit(solution)/shard_map/dot_general | solution.py:93
  204.7 0.0 reduce-scatter.6.cloned.1.call-update
  204.7 0.0 copy-start.4
  204.7 0.0 reduce-scatter.8.cloned.1.call-start
  204.8 0.0 copy-done.2
  204.8 10.6 %fusion.26 = f32[384,1792]{1,0:T(8,128)} fusion(bf16[384,4096]{1,0:T(8,128)(2,1)S(1)} %copy-done.2, bf16[4096,1792]{1,0:T(8,128)(2,1)} %param.25), kind=kOutput, calls=%fused_computation.54 | convolution fusion | flops 5637144576 | bytes 20578304 | tf_op jit(solution)/shard_map/dot_general | solution.py:94
  215.4 0.0 reduce-scatter.8.cloned.1.call-update
  215.5 0.0 copy-done.4
  215.5 0.6 dynamic-slice
  216.1 0.0 copy-start.1
  216.7 0.7 multiply_reduce_fusion
  217.4 5.1 %all-reduce = f32[384]{0:T(512)S(1)} all-reduce(f32[384]{0:T(512)S(1)} %multiply_reduce_fusion), channel_id=4, replica_groups=mesh['grp'=2,'mr'=8,'mc'=2] {'mc'}, use_global_device_ids=true, to_apply=%region_6.9.clone | all-reduce | flops 384 | bytes 3072
  222.6 0.1 fusion.20
  222.7 19.8 %reduce-scatter.6.cloned.1.call-done = f32[192,1792]{1,0:T(8,128)} async-done(((f32[384,1792]{1,0:T(8,128)}), f32[192,1792]{1,0:T(8,128)}) %reduce-scatter.6.cloned.1.call-update) | async-done | bytes 1376272 | tf_op jit(solution)/shard_map/reduce_scatter | solution.py:96
  242.4 41.2 %reduce-scatter.8.cloned.1.call-done = f32[192,1792]{1,0:T(8,128)} async-done(((f32[384,1792]{1,0:T(8,128)}), f32[192,1792]{1,0:T(8,128)}) %reduce-scatter.8.cloned.1.call-update) | async-done | bytes 1376272 | tf_op jit(solution)/shard_map/reduce_scatter | solution.py:97
  283.7 3.1 %multiply_convert_fusion = bf16[192,1792]{1,0:T(8,128)(2,1)} fusion(f32[192,1792]{1,0:T(8,128)} %reduce-scatter.8.cloned.1.call-done, f32[192,1792]{1,0:T(8,128)} %reduce-scatter.6.cloned.1.call-done, f32[192]{0:T(256)S(1)} %fusion.20), kind=kLoop, calls=%fused_computation.16 | loop fusion | flops 2752512 | bytes 3441408 | tf_op jit(solution)/shard_map/convert_element_type | solution.py:103
  286.7 0.0 copy-done.1
  (12 shorter events, 0.2 us)
Async XLA Ops:
  7.2 5.1 %copy-start = (bf16[24,4096]{1,0:T(8,128)(2,1)S(1)}, bf16[24,4096]{1,0:T(8,128)(2,1)}, u32[]{:S(2)}) copy-start(bf16[24,4096]{1,0:T(8,128)(2,1)} %param.15) | copy-start | bytes 589828
  7.2 137.2 %reduce-scatter.4.cloned.1.call-start = ((), (), s32[]{:S(2)}) async-start(), calls=%async_computation.4 | async-start | bytes 6684672 | tf_op jit(solution)/shard_map/reduce_scatter | solution.py:83
  61.4 83.0 %copy-start.3 = (bf16[24,4096]{1,0:T(8,128)(2,1)S(1)}, bf16[24,4096]{1,0:T(8,128)(2,1)}, u32[]{:S(2)}) copy-start(bf16[24,4096]{1,0:T(8,128)(2,1)} %param.22) | copy-start | bytes 589828
  61.4 130.4 %all-gather.2.cloned.1.call-start = ((), (), s32[]{:S(2)}) async-start(), calls=%async_computation.5 | async-start | bytes 3342336 | tf_op jit(solution)/shard_map/all_gather | solution.py:90
  146.1 96.3 %reduce-scatter.6.cloned.1.call-start = ((), (), s32[]{:S(2)}) async-start(), calls=%async_computation.6 | async-start | bytes 4128768 | tf_op jit(solution)/shard_map/reduce_scatter | solution.py:96
  191.8 13.0 %copy-start.2 = (bf16[384,4096]{1,0:T(8,128)(2,1)S(1)}, bf16[384,4096]{1,0:T(8,128)(2,1)}, u32[]{:S(2)}) copy-start(bf16[384,4096]{1,0:T(8,128)(2,1)} %all-gather.2.cloned.1.call-done) | copy-start | bytes 9437188
  204.7 10.7 %copy-start.4 = (u32[32]{0:T(128)S(1)}, u32[32]{0:T(128)}, u32[]{:S(2)}) copy-start(u32[32]{0:T(128)} %constant.77) | copy-start | bytes 388
  204.7 78.9 %reduce-scatter.8.cloned.1.call-start = ((), (), s32[]{:S(2)}) async-start(), calls=%async_computation.7 | async-start | bytes 4128768 | tf_op jit(solution)/shard_map/reduce_scatter | solution.py:97
  216.1 70.7 %copy-start.1 = (bf16[24,4096]{1,0:T(8,128)(2,1)S(1)}, bf16[24,4096]{1,0:T(8,128)(2,1)}, u32[]{:S(2)}) copy-start(bf16[24,4096]{1,0:T(8,128)(2,1)} %param.15) | copy-start | bytes 589828
Sparse Core Ops, SparseCore 0:
  61.5 82.8 reduce-scatter.3
  147.2 44.5 all-gather.1
  204.9 37.5 reduce-scatter.5
  244.5 39.0 reduce-scatter.7
where the time goes:
time: 294 us; the launch traced here: 293 us
  waiting for transfers between devices  190 us (65%)
  matrix products  42.6 us (14%)
  blocking collectives  32.7 us (11%)
  between operations  14.6 us (5%)
  other arithmetic  7.29 us (2%)
  local copies, waits for them, and re-layouts  6.18 us (2%)
    reduce_scatter x1, waiting for transfers between devices, body(): lax.psum_scatter(jnp.dot(features, out_weight, preferred_element_type=jnp...  83 us
    all_gather x1, waiting for transfers between devices, body(): everyone = lax.all_gather(residual_out, ('grp', 'mr'), axis=0, tiled=True)  45.6 us
    reduce_scatter x1, waiting for transfers between devices, body(): lax.psum_scatter(up_term, 'mc', scatter_dimension=0, tiled=True)  41.2 us
    reduce_scatter x1, waiting for transfers between devices, body(): lax.psum_scatter(gate_term, 'mc', scatter_dimension=0, tiled=True)  19.8 us
    all_to_all x1, blocking collectives, body(): lax.all_to_all(gathered, ('grp', 'mr'), split_axis=1, concat_axis=0, tile...  19 us
    dot_general x1, matrix products, body(): jnp.dot(everyone, gate_weight, preferred_element_type=jnp.float32)  12.9 us
    dot_general x1, matrix products, body(): up_term = jnp.dot(everyone, up_weight, preferred_element_type=jnp.float32)  10.6 us
    all_gather x1, blocking collectives, body(): gathered = lax.all_gather(attended, 'mc', axis=1, tiled=True)  8.54 us
  transfers between devices with their start and end apart: 4, of which 4 were waited for; matrix products, arithmetic and copies ran while one was open for 4% of the time, Pallas kernels for 0%

commit v1 on v0

--- a/solution.py
+++ b/solution.py
@@ -80,28 +80,55 @@
     attended = jnp.take(by_cache, device_slot_index, axis=0)
     gathered = lax.all_gather(attended, "mc", axis=1, tiled=True)
     features = lax.all_to_all(gathered, ("grp", "mr"), split_axis=1, concat_axis=0, tiled=True)
+    groups = lax.axis_size("grp")
+    rows = features.shape[0]
+    group_rows = rows // groups
+    group = lax.axis_index("grp")
+    own_share = None
+    for shift in range(groups - 1, -1, -1):
+        target = lax.rem(group + shift, groups)
+        block = lax.dynamic_slice_in_dim(features, target * group_rows, group_rows, axis=0)
+        term = jnp.dot(block, out_weight, preferred_element_type=jnp.float32)
+        if shift > 0:
+            pairs = [(i, (i + shift) % groups) for i in range(groups)]
+            term = lax.ppermute(term.astype(jnp.bfloat16), "grp", pairs).astype(jnp.float32)
+        own_share = term if own_share is None else own_share + term
     shares = lax.psum_scatter(
-        jnp.dot(features, out_weight, preferred_element_type=jnp.float32),
-        ("grp", "mr"),
-        scatter_dimension=0,
-        tiled=True,
-    )
+        own_share.astype(jnp.bfloat16), "mr", scatter_dimension=0, tiled=True
+    ).astype(jnp.float32)
     residual_out = (residual_in.astype(jnp.float32) + shares).astype(jnp.bfloat16)
-    everyone = lax.all_gather(residual_out, ("grp", "mr"), axis=0, tiled=True)
+    group_part = lax.all_gather(residual_out, "mr", axis=0, tiled=True)
+    everyone = lax.all_gather(group_part, "grp", axis=0, tiled=True) if groups != 2 else None
+    if groups == 2:
+        other_part = lax.ppermute(group_part, "grp", [(0, 1), (1, 0)])
+        first = jnp.where(group == 0, group_part, other_part)
+        second = jnp.where(group == 0, other_part, group_part)
+        everyone = jnp.concatenate([first, second], axis=0)
     widened = lax.optimization_barrier(everyone).astype(jnp.float32)
     squares = jnp.sum(widened * widened, axis=1)
+    square_sum = scatter_sum(squares, jnp.float32)
     gate_term = jnp.dot(everyone, gate_weight, preferred_element_type=jnp.float32)
+    gate_sum = scatter_sum(gate_term, jnp.bfloat16)
     up_term = jnp.dot(everyone, up_weight, preferred_element_type=jnp.float32)
-    gate_sum, up_sum, square_sum = (
-        lax.psum_scatter(gate_term, "mc", scatter_dimension=0, tiled=True),
-        lax.psum_scatter(up_term, "mc", scatter_dimension=0, tiled=True),
-        lax.psum_scatter(squares, "mc", scatter_dimension=0, tiled=True),
-    )
+    up_sum = scatter_sum(up_term, jnp.bfloat16)
     inverse_rms = lax.rsqrt(square_sum / D + norm_epsilon)
     gate_value = gate_sum * inverse_rms[:, None]
     upward = up_sum * inverse_rms[:, None]
     activation = (jax.nn.silu(gate_value) * upward).astype(jnp.bfloat16)
     return (residual_out, activation)
+
+
+def scatter_sum(term, kind):
+    count = lax.axis_size("mc")
+    me = lax.axis_index("mc")
+    kept = term.shape[0] // count
+    total = lax.dynamic_slice_in_dim(term, me * kept, kept, axis=0)
+    for shift in range(1, count):
+        target = lax.rem(me + shift, count)
+        sent = lax.dynamic_slice_in_dim(term, target * kept, kept, axis=0).astype(kind)
+        pairs = [(i, (i + shift) % count) for i in range(count)]
+        total = total + lax.ppermute(sent, "mc", pairs).astype(jnp.float32)
+    return total
 
 
 def solution(mesh):

time: 294 us -> 236 us (0.80)
  waiting for transfers between devices: 190 us -> 149 us
  blocking collectives: 32.7 us -> 8.53 us
  starting transfers between devices: 0.16 us -> 9.95 us
  matrix products: 42.6 us -> 36.3 us
    reduce_scatter x3 -> x1, waiting for transfers between devices: 144 us -> 63.5 us  [body(): lax.psum_scatter(own_share.astype(jnp.bfloat16), 'mr', scatter_dimension=...]
    ppermute x0 -> x5, waiting for transfers between devices: none -> 28.4 us  [the longest x3 21.1 us: scatter_sum(): total = total + lax.ppermute(sent, 'mc', pairs).astype(jnp.float32)]
    all_to_all x1 -> x0, blocking collectives: 19 us -> none  [body(): lax.all_to_all(gathered, ('grp', 'mr'), split_axis=1, concat_axis=0, tile...]
    all_to_all x0 -> x1, waiting for transfers between devices: none -> 13 us  [body(): lax.all_to_all(gathered, ('grp', 'mr'), split_axis=1, concat_axis=0, tile...]
    all_to_all x0 -> x1, starting transfers between devices: none -> 6.19 us  [body(): lax.all_to_all(gathered, ('grp', 'mr'), split_axis=1, concat_axis=0, tile...]
    unnamed x1 -> x0, blocking collectives: 5.14 us -> none
    dot_general x1, matrix products: 10.6 us -> 5.86 us  [body(): up_term = jnp.dot(everyone, up_weight, preferred_element_type=jnp.float32)]
    dot_general x1, matrix products: 12.9 us -> 9.31 us  [body(): jnp.dot(everyone, gate_weight, preferred_element_type=jnp.float32)]
  transfers between devices with their start and end apart: 4 -> 8, of which waited for: 4 -> 6; matrix products, arithmetic and copies ran while one was open for 4% -> 3% of each run, Pallas kernels for 0% -> 0%
where the time goes in v1:
time: 236 us
  waiting for transfers between devices  149 us (63%)
  matrix products  36.3 us (15%)
  between operations  14.3 us (6%)
  starting transfers between devices  9.95 us (4%)
  other arithmetic  9.32 us (4%)
  blocking collectives  8.53 us (4%)
  local copies, waits for them, and re-layouts  8.38 us (4%)
    reduce_scatter x1, waiting for transfers between devices, body(): lax.psum_scatter(own_share.astype(jnp.bfloat16), 'mr', scatter_dimension=...  63.5 us
    all_gather x1, waiting for transfers between devices, body(): group_part = lax.all_gather(residual_out, 'mr', axis=0, tiled=True)  44.1 us
    ppermute x3, waiting for transfers between devices, scatter_sum(): total = total + lax.ppermute(sent, 'mc', pairs).astype(jnp.float32)  21.1 us
    all_to_all x1, waiting for transfers between devices, body(): lax.all_to_all(gathered, ('grp', 'mr'), split_axis=1, concat_axis=0, tile...  13 us
    dot_general x1, matrix products, body(): jnp.dot(everyone, gate_weight, preferred_element_type=jnp.float32)  9.31 us
    dot_general x2, matrix products, body(): term = jnp.dot(block, out_weight, preferred_element_type=jnp.float32)  8.72 us
    all_gather x1, blocking collectives, body(): gathered = lax.all_gather(attended, 'mc', axis=1, tiled=True)  8.53 us
    dot_general x1, matrix products, attend_rows(): jnp.einsum('bkgd,bckd->bkgc', query_grouped_four, key_four, preferred_ele...  6.45 us
  transfers between devices with their start and end apart: 8, of which 6 were waited for; matrix products, arithmetic and copies ran while one was open for 3% of the time, Pallas kernels for 0%

profile of v1, /device:TPU:0, one launch (start us, length us, event | category | flops | bytes accessed | tf_op | source)
XLA Modules:
  0.0 235.8 jit_solution(16639397591601032340)
XLA Ops:
  7.2 0.0 copy-start
  7.2 0.7 compare_and_fusion
  7.9 0.1 select_reduce_fusion
  8.0 1.4 gather_fusion
  9.4 1.4 gather_fusion.2
  10.7 1.4 gather_fusion.3
  12.1 0.1 select_convert_fusion
  12.2 0.0 copy-done
  12.2 0.7 gather_fusion.1
  12.9 0.1 select_bitcast_fusion
  13.0 0.1 iota_compare_fusion
  13.1 0.2 fusion.30
  13.3 6.5 %fusion.29 = (f32[24,4,8]{2,1,0:T(4,128)S(1)}, f32[24,4,8,512]{3,2,1,0:T(8,128)S(1)}) fusion(bf16[24,4,8,128]{3,2,1,0:T(8,128)(2,1)S(1)} %bitcast.56, pred[24,512]{1,0:T(8,128)(4,1)S(1)} %iota_compare_fusion, bf16[24,512,512]{2,1,0:T(8,128)(2,1)} %param.18), kind=kOutput, calls=%fused_computation.62 | convolution fusion | flops 101842176 | bytes 14367744 | tf_op jit(solution)/shard_map/bkgd,bckd->bkgc/dot_general | solution.py:26
  19.8 0.5 fusion.8
  20.4 5.8 %fusion.12 = bf16[24,4,8,128]{3,2,1,0:T(8,128)(2,1)S(1)} fusion(f32[24,4,8,512]{3,2,1,0:T(8,128)S(1)} %get-tuple-element.16, f32[24,4,8]{2,1,0:T(4,128)S(1)} %get-tuple-element.11, f32[24,4,8]{2,1,0:T(4,128)S(1)} %multiply_maximum_fusion, f32[24,4,128]{2,1,0:T(4,128)S(1)} %reshape.91, f32[24,4,8]{2,1,0:T(4,128)S(1)} %get-tuple-element.10, ...), kind=kOutput, calls=%fused_computation.25 | convolution fusion | flops 102137856 | bytes 14410752 | tf_op jit(solution)/shard_map/bkgc,bckd->bkgd/dot_general | solution.py:46
  26.2 0.1 copy.47
  26.3 0.7 gather_fusion.4
  27.0 0.1 broadcast_select_fusion.2
  27.1 8.5 %all_gather.6 = bf16[24,8192]{1,0:T(8,128)(2,1)S(1)} all-gather(bf16[24,4096]{1,0:T(8,128)(2,1)S(1)} %broadcast_select_fusion.2), channel_id=1, replica_groups=mesh['grp'=2,'mr'=8,'mc'=2] {'mc'}, dimensions={1}, use_global_device_ids=true | all-gather | bytes 589824 | tf_op jit(solution)/shard_map/all_gather | solution.py:81
  35.6 0.8 copy.46
  36.4 6.2 %all-to-all-start = ((bf16[24,16,512]{2,0,1:T(8,128)(2,1)}), bf16[24,16,512]{2,0,1:T(8,128)(2,1)S(1)}, u32[]{:S(2)}, u32[]{:S(2)}) async-start(bf16[24,16,512]{2,0,1:T(8,128)(2,1)} %bitcast.49), calls=%async_computation | async-start | bytes 786432 | tf_op jit(solution)/shard_map/all_to_all | solution.py:82
  42.5 0.0 reduce-scatter.2.cloned.1.call-start
  42.6 13.0 %all-to-all-done = bf16[24,16,512]{2,0,1:T(8,128)(2,1)S(1)} async-done(((bf16[24,16,512]{2,0,1:T(8,128)(2,1)}), bf16[24,16,512]{2,0,1:T(8,128)(2,1)S(1)}, u32[]{:S(2)}, u32[]{:S(2)}) %all-to-all-start) | async-done | bytes 393248 | tf_op jit(solution)/shard_map/all_to_all | solution.py:82
  55.6 4.4 %convolution_convert_fusion = bf16[192,4096]{1,0:T(8,128)(2,1)} fusion(bf16[512,4096]{1,0:T(8,128)(2,1)} %param.23, bf16[384,512]{1,0:T(8,128)(2,1)S(1)} %bitcast.52, s32[]{:T(128)S(6)} %select_n.80), kind=kOutput, calls=%fused_computation.12 | convolution fusion | flops 806092800 | bytes 5963780 | tf_op jit(solution)/shard_map/dot_general | solution.py:91
  60.0 0.0 collective-permute-start
  60.0 3.6 %collective-permute-done = bf16[192,4096]{1,0:T(8,128)(2,1)S(1)} collective-permute-done((bf16[192,4096]{1,0:T(8,128)(2,1)}, bf16[192,4096]{1,0:T(8,128)(2,1)S(1)}, u32[]{:S(2)}, u32[]{:S(2)}) %collective-permute-start) | collective-permute-done | bytes 1572896 | tf_op jit(solution)/shard_map/ppermute | solution.py:94
  63.6 4.4 %add_convert_fusion = bf16[192,4096]{1,0:T(8,128)(2,1)} fusion(bf16[192,4096]{1,0:T(8,128)(2,1)S(1)} %collective-permute-done, bf16[512,4096]{1,0:T(8,128)(2,1)} %param.23, bf16[384,512]{1,0:T(8,128)(2,1)S(1)} %bitcast.53, s32[]{:T(128)S(6)} %select_n.81), kind=kOutput, calls=%fused_computation.14 | convolution fusion | flops 807665664 | bytes 7536644 | tf_op jit(solution)/shard_map/dot_general | solution.py:91
  67.9 0.0 reduce-scatter.2.cloned.1.call-update
  68.0 0.2 all-gather.2.cloned.1.call-start
  68.2 63.5 %reduce-scatter.2.cloned.1.call-done = bf16[24,4096]{1,0:T(8,128)(2,1)} async-done(((bf16[192,4096]{1,0:T(8,128)(2,1)}), bf16[24,4096]{1,0:T(8,128)(2,1)}) %reduce-scatter.2.cloned.1.call-update) | async-done | bytes 196624 | tf_op jit(solution)/shard_map/reduce_scatter | solution.py:96
  131.7 0.0 copy-done.3
  131.7 1.6 add_convert_fusion.1
  133.3 0.0 all-gather.2.cloned.1.call-update
  133.4 44.1 %all-gather.2.cloned.1.call-done = bf16[192,4096]{1,0:T(8,128)(2,1)} async-done(((bf16[24,4096]{1,0:T(8,128)(2,1)}), bf16[192,4096]{1,0:T(8,128)(2,1)}) %all-gather.2.cloned.1.call-update) | async-done | bytes 1572880 | tf_op jit(solution)/shard_map/all_gather | solution.py:100
  177.5 0.0 collective-permute-start.1
  177.5 3.6 %collective-permute-done.1 = bf16[192,4096]{1,0:T(8,128)(2,1)S(1)} collective-permute-done((bf16[192,4096]{1,0:T(8,128)(2,1)}, bf16[192,4096]{1,0:T(8,128)(2,1)S(1)}, u32[]{:S(2)}, u32[]{:S(2)}) %collective-permute-start.1) | collective-permute-done | bytes 1572896 | tf_op jit(solution)/shard_map/ppermute | solution.py:103
  181.1 0.0 slice-start
  181.1 1.8 broadcast_select_fusion.1
  182.9 0.0 slice-start.1
  182.9 0.0 slice-start.2
  182.9 0.0 slice-start.3
  182.9 9.3 %fusion.28 = f32[384,1792]{1,0:T(8,128)S(1)} fusion(bf16[4096,1792]{1,0:T(8,128)(2,1)} %param.24, bf16[192,4096]{1,0:T(8,128)(2,1)S(1)} %get-tuple-element.9, bf16[192,4096]{1,0:T(8,128)(2,1)S(1)} %get-tuple-element.8), kind=kOutput, calls=%fused_computation.61 | convolution fusion | flops 5643436032 | bytes 20578304 | tf_op jit(solution)/shard_map/dot_general | solution.py:110
  192.2 0.9 dynamic-slice_convert_fusion.1
  193.2 1.5 collective-permute-start.2
  194.6 0.0 slice-done
  194.6 0.0 slice-done.1
  194.6 0.0 slice-done.2
  194.6 0.0 slice-done.3
  194.7 5.9 %fusion.27 = f32[384,1792]{1,0:T(8,128)S(1)} fusion(bf16[4096,1792]{1,0:T(8,128)(2,1)S(1)} %bitcast.61, bf16[192,4096]{1,0:T(8,128)(2,1)S(1)} %get-tuple-element.9, bf16[192,4096]{1,0:T(8,128)(2,1)S(1)} %get-tuple-element.8), kind=kOutput, calls=%fused_computation.60 | convolution fusion | flops 5643436032 | bytes 20578304 | tf_op jit(solution)/shard_map/dot_general | solution.py:112
  200.5 0.0 copy-start.2
  200.5 1.0 dynamic-slice_convert_fusion
  201.5 0.6 collective-permute-start.4
  202.1 0.2 pad_maximum_fusion
  202.3 0.0 copy-done.2
  202.3 0.0 copy-start.1
  202.3 0.7 multiply_reduce_fusion
  203.0 0.1 dynamic_slice.29
  203.1 1.5 collective-permute-start.3
  204.6 21.1 %collective-permute-done.3 = f32[192]{0:T(256)S(1)} collective-permute-done((f32[192]{0:T(256)S(1)}, f32[192]{0:T(256)S(1)}, u32[]{:S(2)}, u32[]{:S(2)}) %collective-permute-start.3) | collective-permute-done | bytes 800 | tf_op jit(solution)/shard_map/ppermute | solution.py:130
  225.7 0.1 add_rsqrt_fusion
  225.8 0.0 collective-permute-done.2
  225.8 0.0 collective-permute-done.4
  225.8 3.2 %multiply_convert_fusion = bf16[192,1792]{1,0:T(8,128)(2,1)} fusion(bf16[192,1792]{1,0:T(8,128)(2,1)} %collective-permute-done.4, f32[384,1792]{1,0:T(8,128)} %copy-done.2, s32[]{:T(128)S(6)} %select_n.85, bf16[192,1792]{1,0:T(8,128)(2,1)} %collective-permute-done.2, f32[384,1792]{1,0:T(8,128)S(1)} %fusion.28, f32[192]{0:T(256)S(1)} %add_rsqrt_fusion), kind=kLoop, calls=%fused_computation.21 | loop fusion | flops 4128768 | bytes 4817668 | tf_op jit(solution)/shard_map/convert_element_type | solution.py:117
  229.0 0.0 copy-done.1
  (12 shorter events, 0.2 us)
Async XLA Ops:
  7.2 5.0 %copy-start = (bf16[24,4096]{1,0:T(8,128)(2,1)S(1)}, bf16[24,4096]{1,0:T(8,128)(2,1)}, u32[]{:S(2)}) copy-start(bf16[24,4096]{1,0:T(8,128)(2,1)} %param.15) | copy-start | bytes 589828
  36.4 19.3 %all-to-all-start = ((bf16[24,16,512]{2,0,1:T(8,128)(2,1)}), bf16[24,16,512]{2,0,1:T(8,128)(2,1)S(1)}, u32[]{:S(2)}, u32[]{:S(2)}) async-start(bf16[24,16,512]{2,0,1:T(8,128)(2,1)} %bitcast.49), calls=%async_computation | async-start | bytes 786432 | tf_op jit(solution)/shard_map/all_to_all | solution.py:82
  42.5 89.1 %reduce-scatter.2.cloned.1.call-start = ((), (), s32[]{:S(2)}) async-start(), calls=%async_computation.2 | async-start | bytes 1769472 | tf_op jit(solution)/shard_map/reduce_scatter | solution.py:96
  60.0 3.6 %collective-permute-start = (bf16[192,4096]{1,0:T(8,128)(2,1)}, bf16[192,4096]{1,0:T(8,128)(2,1)S(1)}, u32[]{:S(2)}, u32[]{:S(2)}) collective-permute-start(bf16[192,4096]{1,0:T(8,128)(2,1)} %convolution_convert_fusion), channel_id=1, source_target_pairs={{0,16},{16,0},{1,17},{17,1},{2,18},{18,2},{3,19},{19,3},{4,20},{20... | collective-permute-start | bytes 4718600 | tf_op jit(solution)/shard_map/ppermute | solution.py:94
  60.0 71.7 %copy-start.3 = (bf16[24,4096]{1,0:T(8,128)(2,1)S(1)}, bf16[24,4096]{1,0:T(8,128)(2,1)}, u32[]{:S(2)}) copy-start(bf16[24,4096]{1,0:T(8,128)(2,1)} %param.22) | copy-start | bytes 589828
  68.0 109.5 %all-gather.2.cloned.1.call-start = ((), (), s32[]{:S(2)}) async-start(), calls=%async_computation.3 | async-start | bytes 1769472 | tf_op jit(solution)/shard_map/all_gather | solution.py:100
  177.5 3.6 %collective-permute-start.1 = (bf16[192,4096]{1,0:T(8,128)(2,1)}, bf16[192,4096]{1,0:T(8,128)(2,1)S(1)}, u32[]{:S(2)}, u32[]{:S(2)}) collective-permute-start(bf16[192,4096]{1,0:T(8,128)(2,1)} %all-gather.2.cloned.1.call-done), channel_id=1, source_target_pairs={{0,16},{16,0},{1,17},{17,1},{2,18},{18,2},{3,19},{19,3},{4,20},{20... | collective-permute-start | bytes 4718600 | tf_op jit(solution)/shard_map/ppermute | solution.py:103
  181.1 13.5 %slice-start = ((s8[14680064]{0:T(1024)(128)(4,1)}), s8[4194304]{0:T(1024)(128)(4,1)S(1)}, s32[]{:S(2)}) async-start(s8[14680064]{0:T(1024)(128)(4,1)} %bitcast.60), calls=%async_computation.4 | async-start | bytes 8388608
  182.9 11.7 %slice-start.1 = ((s8[14680064]{0:T(1024)(128)(4,1)}), s8[4194304]{0:T(1024)(128)(4,1)S(1)}, s32[]{:S(2)}) async-start(s8[14680064]{0:T(1024)(128)(4,1)} %bitcast.60), calls=%async_computation.5 | async-start | bytes 8388608
  182.9 11.7 %slice-start.2 = ((s8[14680064]{0:T(1024)(128)(4,1)}), s8[4194304]{0:T(1024)(128)(4,1)S(1)}, s32[]{:S(2)}) async-start(s8[14680064]{0:T(1024)(128)(4,1)} %bitcast.60), calls=%async_computation.6 | async-start | bytes 8388608
  182.9 11.7 %slice-start.3 = ((s8[14680064]{0:T(1024)(128)(4,1)}), s8[2097152]{0:T(1024)(128)(4,1)S(1)}, s32[]{:S(2)}) async-start(s8[14680064]{0:T(1024)(128)(4,1)} %bitcast.60), calls=%async_computation.7 | async-start | bytes 4194304
  193.2 32.6 %collective-permute-start.2 = (bf16[192,1792]{1,0:T(8,128)(2,1)}, bf16[192,1792]{1,0:T(8,128)(2,1)}, u32[]{:S(2)}, u32[]{:S(2)}) collective-permute-start(bf16[192,1792]{1,0:T(8,128)(2,1)} %dynamic-slice_convert_fusion.1), channel_id=1, source_target_pairs={{0,1},{1,0},{2,3},{3,2},{4,5},{5,4},{6,7},{7,6},{8,9},{9,8},{10,11... | collective-permute-start | bytes 2064392 | tf_op jit(solution)/shard_map/ppermute | solution.py:130
  200.5 1.8 copy-start.2
  201.5 24.3 %collective-permute-start.4 = (bf16[192,1792]{1,0:T(8,128)(2,1)}, bf16[192,1792]{1,0:T(8,128)(2,1)}, u32[]{:S(2)}, u32[]{:S(2)}) collective-permute-start(bf16[192,1792]{1,0:T(8,128)(2,1)} %dynamic-slice_convert_fusion), channel_id=1, source_target_pairs={{0,1},{1,0},{2,3},{3,2},{4,5},{5,4},{6,7},{7,6},{8,9},{9,8},{10,11... | collective-permute-start | bytes 2064392 | tf_op jit(solution)/shard_map/ppermute | solution.py:130
  202.3 26.7 %copy-start.1 = (bf16[24,4096]{1,0:T(8,128)(2,1)S(1)}, bf16[24,4096]{1,0:T(8,128)(2,1)}, u32[]{:S(2)}) copy-start(bf16[24,4096]{1,0:T(8,128)(2,1)} %param.15) | copy-start | bytes 589828
  203.1 22.6 %collective-permute-start.3 = (f32[192]{0:T(256)S(1)}, f32[192]{0:T(256)S(1)}, u32[]{:S(2)}, u32[]{:S(2)}) collective-permute-start(f32[192]{0:T(256)S(1)} %dynamic_slice.29), channel_id=1, source_target_pairs={{0,1},{1,0},{2,3},{3,2},{4,5},{5,4},{6,7},{7,6},{8,9},{9,8},{10,11... | collective-permute-start | bytes 2312 | tf_op jit(solution)/shard_map/ppermute | solution.py:130
Sparse Core Ops, SparseCore 0:
  68.1 63.5 reduce-scatter.1
  134.5 43.0 all-gather.1
